TPU v7x, 32 devices: a whole 2x2x4 slice. The times are simulated.
32 devices in a mesh: groups: 2 (over y), dp: 4 (over z), heads: 4 (over x, core).
Axes of the slice: x: 2, y: 2, z: 4, core: 2. Of those that a mesh axis runs over, the one named last changes fastest.
Arguments:
- queries: bfloat16 [2048, 64, 128], P(('groups', 'dp'), 'heads'), parts along dimension 0, may hold values from -41 to 41
- out_grad: bfloat16 [2048, 64, 128], P(('groups', 'dp'), 'heads'), parts along dimension 0, may hold values from -24 to 24
- self_keys: bfloat16 [2048, 8, 128], P(('groups', 'dp'), 'heads'), parts along dimension 0, may hold values from -6 to 6
- self_values: bfloat16 [2048, 8, 128], P(('groups', 'dp'), 'heads'), parts along dimension 0, may hold values from -6 to 6
- cart_keys: bfloat16 [2048, 8, 128], P('groups', 'heads'), parts along dimension 0, may hold values from -17 to 17
- cart_values: bfloat16 [2048, 8, 128], P('groups', 'heads'), parts along dimension 0, may hold values from -6 to 6
- segment_ids: int32 [8, 256], P(('groups', 'dp')), parts along dimension 0, may hold values from 0 to 1, never falling along the last dimension, each value on 1 to 192 neighbouring positions
Outputs:
- cart_grads: float32 [2048, 2, 8, 128], P(('groups', 'dp'), None, 'heads'), parts along dimension 0
- self_grads: bfloat16 [2, 2048, 8, 128], P(None, ('groups', 'dp'), 'heads'), parts along dimension 1
- query_grads: bfloat16 [2048, 8192], P(('groups', 'dp', 'heads')), parts along dimension 0
There are 2 independent parts, one for each index of `groups`. A program takes and returns all parts, laid end to end along the dimension named above; each array names one. Nothing has to cross between parts.
Inputs may be any that keep to these rules, and one draw needn't show every extreme that they name: `segment_ids`: in each row ids never fall and both sequences occur; one sequence of a row may hold up to 192 positions.
All inputs are finite; a program needn't handle non-finite values.
Results may differ from a plain program's by a relative error of at most 0.0053.
Values may be sent and summed in bfloat16 or wider, within the bound.
A program may use at most 64 MiB of HBM per device.

v0:
```python
import functools
import math

import jax
import jax.numpy as jnp
from jax import lax
from jax.experimental import pallas as pl
from jax.experimental.pallas import tpu as pltpu
from jax.sharding import PartitionSpec as P

F32 = jnp.float32
BF16 = jnp.bfloat16
MASKED = -1e30
MESH = pl.DeviceIdType.MESH


def nt(a, b):
    return lax.dot_general(a, b, (((1,), (1,)), ((), ())), preferred_element_type=F32)


def tn(a, b):
    return lax.dot_general(a, b, (((0,), (0,)), ((), ())), preferred_element_type=F32)


def kernel(
    ndp, nh,
    seg_col, seg_row, q_ref, g_ref, k_ref, v_ref,
    dq_out, cart_out, self_out,
    bias, p_scr, ds_scr, dq_buf, stage, land,
    dq_send, dq_recv, dq_loc, rs_send, rs_recv,
):
    heads, tok, dim = q_ref.shape
    kvs, keys, _ = k_ref.shape
    cart = keys - tok
    width = heads // kvs
    share = cart // ndp
    piece = tok // nh
    scale = dim ** -0.5
    expo = scale * math.log2(math.e)
    my_dp = lax.axis_index("dp")
    my_h = lax.axis_index("heads")

    barrier = pltpu.get_barrier_semaphore()

    def greet_dp(i, c):
        pl.semaphore_signal(barrier, inc=1, device_id={"dp": lax.rem(my_dp + i, ndp)}, device_id_type=MESH)
        return c

    def greet_h(i, c):
        pl.semaphore_signal(barrier, inc=1, device_id={"heads": lax.rem(my_h + i, nh)}, device_id_type=MESH)
        return c

    lax.fori_loop(1, ndp, greet_dp, 0)
    lax.fori_loop(1, nh, greet_h, 0)
    pl.semaphore_wait(barrier, ndp - 1 + nh - 1)

    u_pos = lax.broadcasted_iota(jnp.int32, (tok, tok), 0)
    t_pos = lax.broadcasted_iota(jnp.int32, (tok, tok), 1)
    seen = (seg_col[...] == seg_row[...]) & (u_pos <= t_pos)
    bias[...] = jnp.where(seen, 0.0, MASKED)

    def dq_copy(kv, i):
        to = lax.rem(my_h + i, nh)
        cols = width * dim
        return pltpu.make_async_remote_copy(
            src_ref=dq_buf.at[pl.ds(pl.multiple_of(to * piece, piece), piece), pl.ds(kv * cols, cols)],
            dst_ref=dq_out.at[:, pl.ds(pl.multiple_of(my_h * heads * dim + kv * cols, cols), cols)],
            send_sem=dq_send.at[kv, i - 1],
            recv_sem=dq_recv.at[kv, i - 1],
            device_id={"heads": to},
            device_id_type=MESH,
        )

    def dq_arrival(kv, i):
        source = lax.rem(my_h - i + nh, nh)
        cols = width * dim
        landed = dq_out.at[:, pl.ds(pl.multiple_of(source * heads * dim + kv * cols, cols), cols)]
        return pltpu.make_async_remote_copy(
            src_ref=landed, dst_ref=landed,
            send_sem=dq_send.at[kv, i - 1],
            recv_sem=dq_recv.at[kv, i - 1],
            device_id={"heads": source},
            device_id_type=MESH,
        )

    def dq_own(kv):
        cols = width * dim
        return pltpu.make_async_copy(
            dq_buf.at[pl.ds(pl.multiple_of(my_h * piece, piece), piece), pl.ds(kv * cols, cols)],
            dq_out.at[:, pl.ds(pl.multiple_of(my_h * heads * dim + kv * cols, cols), cols)],
            dq_loc.at[kv],
        )

    def rs_copy(kv, i):
        return pltpu.make_async_remote_copy(
            src_ref=stage.at[kv, i - 1],
            dst_ref=land.at[kv, i - 1],
            send_sem=rs_send.at[kv, i - 1],
            recv_sem=rs_recv.at[kv, i - 1],
            device_id={"dp": lax.rem(my_dp + i, ndp)},
            device_id_type=MESH,
        )

    for kv in range(kvs):
        def one_head(j, c, kv=kv):
            h = kv * width + j
            qh = q_ref[h]
            gh = g_ref[h]
            s = nt(k_ref[kv], qh)
            s_cart = s[:cart]
            s_own = s[cart:] + bias[...]
            peak = jnp.maximum(
                jnp.max(s_cart, axis=0, keepdims=True), jnp.max(s_own, axis=0, keepdims=True)
            )
            e_cart = jnp.exp2((s_cart - peak) * expo)
            e_own = jnp.exp2((s_own - peak) * expo)
            total = jnp.sum(e_cart, axis=0, keepdims=True) + jnp.sum(e_own, axis=0, keepdims=True)
            dp = nt(v_ref[kv], gh)
            inverse = 1.0 / total
            center = (
                jnp.sum(e_cart * dp[:cart], axis=0, keepdims=True)
                + jnp.sum(e_own * dp[cart:], axis=0, keepdims=True)
            ) * inverse
            at = pl.ds(pl.multiple_of(j * tok, tok), tok)
            p_cart = e_cart * inverse
            p_own = e_own * inverse
            p_scr[:cart, at] = p_cart.astype(BF16)
            p_scr[cart:, at] = p_own.astype(BF16)
            ds_cart = (p_cart * (dp[:cart] - center)).astype(BF16)
            ds_own = (p_own * (dp[cart:] - center)).astype(BF16)
            ds_scr[:cart, at] = ds_cart
            ds_scr[cart:, at] = ds_own
            dq = tn(ds_scr[:, at], k_ref[kv]) * scale
            dq_buf[:, pl.ds(pl.multiple_of(h * dim, dim), dim)] = dq.astype(BF16)
            return c

        lax.fori_loop(0, width, one_head, 0)

        dq_own(kv).start()

        def send_dq(i, c, kv=kv):
            dq_copy(kv, i).start()
            return c

        lax.fori_loop(1, nh, send_dq, 0)

        q_rows = q_ref[kv * width : (kv + 1) * width].reshape(width * tok, dim)
        g_rows = g_ref[kv * width : (kv + 1) * width].reshape(width * tok, dim)

        def key_block(rows):
            dk = jnp.dot(ds_scr[rows, :], q_rows, preferred_element_type=F32) * scale
            dv = jnp.dot(p_scr[rows, :], g_rows, preferred_element_type=F32)
            return dk, dv

        def send_share(i, c, kv=kv, key_block=key_block):
            to = lax.rem(my_dp + i, ndp)
            dk, dv = key_block(pl.ds(pl.multiple_of(to * share, share), share))
            stage[kv, i - 1, 0] = dk.astype(BF16)
            stage[kv, i - 1, 1] = dv.astype(BF16)
            rs_copy(kv, i).start()
            return c

        lax.fori_loop(1, ndp, send_share, 0)
        dk, dv = key_block(pl.ds(pl.multiple_of(my_dp * share, share), share))
        cart_out[kv, 0] = dk
        cart_out[kv, 1] = dv
        dk, dv = key_block(pl.ds(cart, tok))
        self_out[0, kv] = dk.astype(BF16)
        self_out[1, kv] = dv.astype(BF16)

    for kv in range(kvs):
        dq_own(kv).wait()

        def end_dq(i, c, kv=kv):
            dq_copy(kv, i).wait_send()
            dq_arrival(kv, i).wait_recv()
            return c

        lax.fori_loop(1, nh, end_dq, 0)

        def end_rs(i, c, kv=kv):
            rs_copy(kv, i).wait_send()
            rs_copy(kv, i).wait_recv()
            cart_out[kv] += land[kv, i - 1].astype(F32)
            return c

        lax.fori_loop(1, ndp, end_rs, 0)


def on_device(ndp, nh, queries, out_grad, self_keys, self_values, cart_keys, cart_values, segment_ids):
    tok, heads, dim = queries.shape
    kvs = self_keys.shape[1]
    cart = cart_keys.shape[0]
    keys = cart + tok
    width = heads // kvs
    share = cart // ndp
    piece = tok // nh
    q = queries.transpose(1, 0, 2)
    g = out_grad.transpose(1, 0, 2)
    k = jnp.concatenate([cart_keys, self_keys], axis=0).transpose(1, 0, 2)
    v = jnp.concatenate([cart_values, self_values], axis=0).transpose(1, 0, 2)
    vmem = pl.BlockSpec(memory_space=pltpu.VMEM)
    dma = pltpu.SemaphoreType.DMA
    query_grads, cart_part, self_part = pl.pallas_call(
        functools.partial(kernel, ndp, nh),
        out_shape=(
            jax.ShapeDtypeStruct((piece, nh * heads * dim), BF16),
            jax.ShapeDtypeStruct((kvs, 2, share, dim), F32),
            jax.ShapeDtypeStruct((2, kvs, tok, dim), BF16),
        ),
        in_specs=[vmem] * 6,
        out_specs=(pl.BlockSpec(memory_space=pl.ANY), vmem, vmem),
        scratch_shapes=[
            pltpu.VMEM((tok, tok), F32),
            pltpu.VMEM((keys, width * tok), BF16),
            pltpu.VMEM((keys, width * tok), BF16),
            pltpu.VMEM((tok, heads * dim), BF16),
            pltpu.VMEM((kvs, ndp - 1, 2, share, dim), BF16),
            pltpu.VMEM((kvs, ndp - 1, 2, share, dim), BF16),
            dma((kvs, nh - 1)),
            dma((kvs, nh - 1)),
            dma((kvs,)),
            dma((kvs, ndp - 1)),
            dma((kvs, ndp - 1)),
        ],
        compiler_params=pltpu.CompilerParams(
            collective_id=0, has_side_effects=True, vmem_limit_bytes=60 << 20
        ),
        name="attention_backward",
    )(segment_ids.reshape(tok, 1), segment_ids.reshape(1, tok), q, g, k, v)
    cart_grads = cart_part.transpose(2, 1, 0, 3)
    self_grads = self_part.transpose(0, 2, 1, 3)
    return cart_grads, self_grads, query_grads


def solution(mesh):
    in_specs = (
        P(("groups", "dp"), "heads", None),
        P(("groups", "dp"), "heads", None),
        P(("groups", "dp"), "heads", None),
        P(("groups", "dp"), "heads", None),
        P("groups", "heads", None),
        P("groups", "heads", None),
        P(("groups", "dp"), None),
    )
    out_specs = (
        P(("groups", "dp"), None, "heads", None),
        P(None, ("groups", "dp"), "heads", None),
        P(("groups", "dp", "heads"), None),
    )
    body = functools.partial(on_device, mesh.shape["dp"], mesh.shape["heads"])
    return jax.shard_map(body, mesh=mesh, in_specs=in_specs, out_specs=out_specs, check_vma=False)
```

profile of v0, /device:TPU:0, one launch (start us, length us, event | category | flops | bytes accessed | tf_op | source)
XLA Modules:
  0.0 65.4 jit_solution(14143436360678974633)
XLA Ops:
  0.6 0.0 copy-start.3
  0.6 1.0 %copy.21 = bf16[256,2,128]{2,0,1:T(8,128)(2,1)S(1)} copy(bf16[256,2,128]{2,1,0:T(2,128)(2,1)} %param.9) | data formatting | bytes 262144 | tf_op args[2]
  1.6 0.9 %copy.23 = bf16[256,2,128]{2,0,1:T(8,128)(2,1)S(1)} copy(bf16[256,2,128]{2,1,0:T(2,128)(2,1)} %param.10) | data formatting | bytes 262144 | tf_op args[3]
  2.6 1.5 %copy.24.seg_col = s32[256,1]{1,0:T(8,128)} copy(s32[256,1]{0,1:T(1,128)} %bitcast.13) | data formatting | bytes 2048 | tf_op jit(solution)/shard_map/reshape | solution.py:230
  4.0 1.1 %copy.20 = bf16[1024,2,128]{2,0,1:T(8,128)(2,1)S(1)} copy(bf16[1024,2,128]{2,1,0:T(2,128)(2,1)} %param.11) | data formatting | bytes 1048576 | tf_op args[4]
  5.1 0.0 copy-done.3
  5.2 0.1 copy.22
  5.2 0.0 copy-start.1
  5.2 0.0 copy-start.2
  5.3 1.2 %maximum_bitcast_fusion = (bf16[2,1280,128]{2,1,0:T(8,128)(2,1)}, bf16[2,1280,128]{2,1,0:T(8,128)(2,1)}) fusion(bf16[256,2,128]{2,0,1:T(8,128)(2,1)S(1)} %copy.21, bf16[1024,2,128]{2,0,1:T(8,128)(2,1)S(1)} %copy.20, bf16[256,2,128]{2,0,1:T(8,128)(2,1)S(1)} %copy.23, bf16[1024,2,128]{2,0,1:T(8,128)(2,1)S(1)} %copy.22), kind=kLoop, calls=%fused_computation.2 | loop fusion | flops 2621440 | bytes 2621440 | tf_op jit(solution)/shard_map/transpose | solution.py:200
  6.4 0.5 copy-done.1
  6.9 0.3 copy-done.2
  7.2 1.9 %copy_bitcast_fusion = (bf16[16,256,128]{2,1,0:T(8,128)(2,1)}, bf16[16,256,128]{2,1,0:T(8,128)(2,1)}) fusion(bf16[256,16,128]{2,1,0:T(8,128)(2,1)S(1)} %copy-done.1, bf16[256,16,128]{2,1,0:T(8,128)(2,1)S(1)} %copy-done.2), kind=kLoop, calls=%fused_computation | loop fusion | bytes 4194304 | tf_op jit(solution)/shard_map/transpose | solution.py:199
  9.2 51.0 %attention_backward.1 = (bf16[64,8192]{1,0:T(8,128)(2,1)}, f32[2,2,256,128]{3,2,1,0:T(8,128)}, bf16[2,2,256,128]{3,2,1,0:T(8,128)(2,1)}) custom-call(s32[256,1]{1,0:T(8,128)} %copy.24.seg_col, s32[1,256]{1,0:T(1,128)} %seg_row.1, bf16[16,256,128]{2,1,0:T(8,128)(2,1)} %get-tuple-element.16.q_ref, bf16[16,256,128]{2,1,0:T(8,128)(2,1)} %get-tuple-element.15.g_ref, ...), custom_call_target="tpu_custom_call" | custom-call | tf_op jit(solution)/shard_map/attention_backward/pallas_call | solution.py:204
  60.2 0.0 copy-start
  60.2 2.3 %copy.25 = f32[256,2,2,128]{3,2,1,0:T(2,128)} copy(f32[256,2,2,128]{3,0,1,2:T(8,128)} %bitcast.11) | data formatting | bytes 1048576
  62.5 1.9 %copy.26 = bf16[2,256,2,128]{3,2,1,0:T(2,128)(2,1)} copy(bf16[2,256,2,128]{3,1,2,0:T(8,128)(2,1)} %bitcast.12) | data formatting | bytes 524288
  64.4 0.0 copy-done
  64.4 1.0 %copy.30 = bf16[64,8192]{1,0:T(8,128)(2,1)} copy(bf16[64,8192]{1,0:T(8,128)(2,1)S(1)} %copy-done) | data formatting | bytes 2097152
Async XLA Ops:
  0.6 4.5 %copy-start.3 = (bf16[1024,2,128]{2,1,0:T(2,128)(2,1)S(1)}, bf16[1024,2,128]{2,1,0:T(2,128)(2,1)}, u32[]{:S(2)}) copy-start(bf16[1024,2,128]{2,1,0:T(2,128)(2,1)} %param.12) | copy-start | bytes 1572868
  5.2 1.7 %copy-start.1 = (bf16[256,16,128]{2,1,0:T(8,128)(2,1)S(1)}, bf16[256,16,128]{2,1,0:T(8,128)(2,1)}, u32[]{:S(2)}) copy-start(bf16[256,16,128]{2,1,0:T(8,128)(2,1)} %param.8) | copy-start | bytes 3145732
  5.2 2.0 %copy-start.2 = (bf16[256,16,128]{2,1,0:T(8,128)(2,1)S(1)}, bf16[256,16,128]{2,1,0:T(8,128)(2,1)}, u32[]{:S(2)}) copy-start(bf16[256,16,128]{2,1,0:T(8,128)(2,1)} %param.7) | copy-start | bytes 3145732
  60.2 4.3 %copy-start = (bf16[64,8192]{1,0:T(8,128)(2,1)S(1)}, bf16[64,8192]{1,0:T(8,128)(2,1)}, u32[]{:S(2)}) copy-start(bf16[64,8192]{1,0:T(8,128)(2,1)} %get-tuple-element.24) | copy-start | bytes 3145732
where the time goes:
time: 65.7 us; the launch traced here: 65.4 us
  Pallas kernels  51 us (78%)
  local copies, waits for them, and re-layouts  12.6 us (19%)
  other arithmetic  1.16 us (2%)
  between operations  0.7 us (1%)
    pallas_call x1, Pallas kernels, on_device(): pl.pallas_call(functools.partial(kernel, ndp, nh), out_shape=(jax.ShapeDt...  51 us
    unnamed x15, local copies, waits for them, and re-layouts  9.16 us
    transpose x1, local copies, waits for them, and re-layouts, on_device(): g = out_grad.transpose(1, 0, 2)  1.94 us
    reshape x1, local copies, waits for them, and re-layouts, on_device(): segment_ids.reshape(tok, 1)  1.48 us

commit v1 on v0

v1 whole, which is shorter than its diff:
```python
import functools
import math

import jax
import jax.numpy as jnp
from jax import lax
from jax.experimental import pallas as pl
from jax.experimental.pallas import tpu as pltpu
from jax.sharding import PartitionSpec as P

F32 = jnp.float32
BF16 = jnp.bfloat16
MASKED = -1e30
MESH = pl.DeviceIdType.MESH


def nt(a, b):
    return lax.dot_general(a, b, (((1,), (1,)), ((), ())), preferred_element_type=F32)


def tn(a, b):
    return lax.dot_general(a, b, (((0,), (0,)), ((), ())), preferred_element_type=F32)


def kernel(
    ndp, nh, kvs,
    seg_ref, q_ref, g_ref, ck_ref, cv_ref, sk_ref, sv_ref,
    dq_out, cart_out, self_out,
    bias, k_scr, v_scr, wide, s_a, d_a, m_a, w_a, s_b, d_b, m_b, w_b,
    p_scr, ds_scr, dq_buf, stage, land, cart_acc, self_acc,
    dq_send, dq_recv, dq_loc, rs_send, rs_recv,
):
    tok, heads, dim = q_ref.shape
    cart = ck_ref.shape[0] // kvs
    keys = cart + tok
    width = heads // kvs
    share = cart // ndp
    piece = tok // nh
    step = s_a.shape[1]
    span = step // width
    blocks = tok // span
    chunk = 128
    scale = dim ** -0.5
    expo = scale * math.log2(math.e)
    my_dp = lax.axis_index("dp")
    my_h = lax.axis_index("heads")

    barrier = pltpu.get_barrier_semaphore()

    def greet_dp(i, c):
        pl.semaphore_signal(barrier, inc=1, device_id={"dp": lax.rem(my_dp + i, ndp)}, device_id_type=MESH)
        return c

    def greet_h(i, c):
        pl.semaphore_signal(barrier, inc=1, device_id={"heads": lax.rem(my_h + i, nh)}, device_id_type=MESH)
        return c

    lax.fori_loop(1, ndp, greet_dp, 0)
    lax.fori_loop(1, nh, greet_h, 0)

    def split_heads(src, dst, base):
        rows = src.shape[0] // kvs
        if kvs == 1:
            dst[0, pl.ds(base, rows)] = src[...]
            return
        wide[: rows * kvs] = src[...].astype(F32)
        for kv in range(kvs):
            dst[kv, pl.ds(base, rows)] = wide[pl.ds(kv, rows, stride=kvs)].astype(BF16)

    split_heads(ck_ref, k_scr, 0)
    split_heads(sk_ref, k_scr, cart)
    split_heads(cv_ref, v_scr, 0)
    split_heads(sv_ref, v_scr, cart)

    seg_u = jnp.broadcast_to(seg_ref[...], (tok, tok))
    seg_t = seg_u.T
    t_pos = lax.broadcasted_iota(jnp.int32, (tok, tok), 0)
    u_pos = lax.broadcasted_iota(jnp.int32, (tok, tok), 1)
    seen = jnp.where((seg_u == seg_t) & (u_pos <= t_pos), 1.0, 0.0).astype(BF16)
    spread = jnp.where(
        lax.broadcasted_iota(jnp.int32, (span, step), 1) // width
        == lax.broadcasted_iota(jnp.int32, (span, step), 0),
        1.0, 0.0,
    ).astype(BF16)
    for b in range(blocks):
        bias[b] = (tn(seen[b * span : (b + 1) * span], spread) - 1.0) * -MASKED

    def rows_of(ref, kv, b):
        heads_at = pl.ds(pl.multiple_of(kv * width, width), width)
        return ref[pl.ds(b * span, span), heads_at, :].reshape(step, dim)

    def score(kv, b, s_x, d_x, m_x):
        qb = rows_of(q_ref, kv, b)
        gb = rows_of(g_ref, kv, b)
        peak = None
        for lo in range(0, keys, chunk):
            s = nt(k_scr[kv, lo : lo + chunk], qb)
            if lo >= cart:
                s = s + bias[b, lo - cart : lo - cart + chunk]
            s_x[lo : lo + chunk] = s
            top = jnp.max(s.reshape(chunk // 8, 8, step), axis=0)
            peak = top if peak is None else jnp.maximum(peak, top)
            d_x[lo : lo + chunk] = nt(v_scr[kv, lo : lo + chunk], gb)
        m_x[...] = jnp.broadcast_to(jnp.max(peak, axis=0, keepdims=True), (8, step))

    def backward(kv, b, s_x, d_x, m_x, w_x):
        peak = m_x[:1]
        total = jnp.zeros((8, step), F32)
        mixed = jnp.zeros((8, step), F32)
        for lo in range(0, keys, chunk):
            e = jnp.exp2((s_x[lo : lo + chunk] - peak) * expo)
            s_x[lo : lo + chunk] = e
            total = total + jnp.sum(e.reshape(chunk // 8, 8, step), axis=0)
            ed = e * d_x[lo : lo + chunk]
            mixed = mixed + jnp.sum(ed.reshape(chunk // 8, 8, step), axis=0)
        inverse = 1.0 / jnp.sum(total, axis=0, keepdims=True)
        center = jnp.sum(mixed, axis=0, keepdims=True) * inverse
        at = pl.ds(pl.multiple_of(b * step, step), step)
        for lo in range(0, keys, chunk):
            p = s_x[lo : lo + chunk] * inverse
            p_scr[lo : lo + chunk, at] = p.astype(BF16)
            ds_scr[lo : lo + chunk, at] = (p * (d_x[lo : lo + chunk] - center)).astype(BF16)
        w_x[...] = tn(ds_scr[:, at], k_scr[kv]) * scale
        rows = pl.ds(pl.multiple_of(b * span, span), span)
        for hh in range(width):
            out = w_x[pl.ds(hh, span, stride=width)].astype(BF16)
            dq_buf[rows, kv * cols + hh * dim : kv * cols + (hh + 1) * dim] = out

    cols = width * dim

    def dq_copy(kv, i):
        to = lax.rem(my_h + i, nh)
        return pltpu.make_async_remote_copy(
            src_ref=dq_buf.at[pl.ds(pl.multiple_of(to * piece, piece), piece), pl.ds(kv * cols, cols)],
            dst_ref=dq_out.at[:, pl.ds(pl.multiple_of(my_h * heads * dim + kv * cols, cols), cols)],
            send_sem=dq_send.at[kv, i - 1],
            recv_sem=dq_recv.at[kv, i - 1],
            device_id={"heads": to},
            device_id_type=MESH,
        )

    def dq_arrival(kv, i):
        source = lax.rem(my_h - i + nh, nh)
        landed = dq_out.at[:, pl.ds(pl.multiple_of(source * heads * dim + kv * cols, cols), cols)]
        return pltpu.make_async_remote_copy(
            src_ref=landed, dst_ref=landed,
            send_sem=dq_send.at[kv, i - 1],
            recv_sem=dq_recv.at[kv, i - 1],
            device_id={"heads": source},
            device_id_type=MESH,
        )

    def dq_own(kv):
        return pltpu.make_async_copy(
            dq_buf.at[pl.ds(pl.multiple_of(my_h * piece, piece), piece), pl.ds(kv * cols, cols)],
            dq_out.at[:, pl.ds(pl.multiple_of(my_h * heads * dim + kv * cols, cols), cols)],
            dq_loc.at[kv],
        )

    def rs_copy(kv, i):
        return pltpu.make_async_remote_copy(
            src_ref=stage.at[kv, i - 1],
            dst_ref=land.at[kv, i - 1],
            send_sem=rs_send.at[kv, i - 1],
            recv_sem=rs_recv.at[kv, i - 1],
            device_id={"dp": lax.rem(my_dp + i, ndp)},
            device_id_type=MESH,
        )

    score(0, 0, s_a, d_a, m_a)
    pl.semaphore_wait(barrier, ndp - 1 + nh - 1)

    for kv in range(kvs):
        def two_blocks(i, c, kv=kv):
            score(kv, 2 * i + 1, s_b, d_b, m_b)
            backward(kv, 2 * i, s_a, d_a, m_a, w_a)
            after = kv * blocks + 2 * i + 2
            score(jnp.minimum(after // blocks, kvs - 1), lax.rem(after, blocks), s_a, d_a, m_a)
            backward(kv, 2 * i + 1, s_b, d_b, m_b, w_b)
            return c

        lax.fori_loop(0, blocks // 2, two_blocks, 0)

        dq_own(kv).start()

        def send_dq(i, c, kv=kv):
            dq_copy(kv, i).start()
            return c

        lax.fori_loop(1, nh, send_dq, 0)

        q_rows = q_ref[:, kv * width : (kv + 1) * width, :].reshape(width * tok, dim)
        g_rows = g_ref[:, kv * width : (kv + 1) * width, :].reshape(width * tok, dim)

        def key_block(rows):
            dk = jnp.dot(ds_scr[rows, :], q_rows, preferred_element_type=F32) * scale
            dv = jnp.dot(p_scr[rows, :], g_rows, preferred_element_type=F32)
            return dk, dv

        def send_share(i, c, kv=kv, key_block=key_block):
            to = lax.rem(my_dp + i, ndp)
            dk, dv = key_block(pl.ds(pl.multiple_of(to * share, share), share))
            stage[kv, i - 1, 0] = dk.astype(BF16)
            stage[kv, i - 1, 1] = dv.astype(BF16)
            rs_copy(kv, i).start()
            return c

        lax.fori_loop(1, ndp, send_share, 0)
        dk, dv = key_block(pl.ds(pl.multiple_of(my_dp * share, share), share))
        cart_acc[kv, 0] = dk
        cart_acc[kv, 1] = dv
        dk, dv = key_block(pl.ds(cart, tok))
        self_acc[pl.ds(kv, tok, stride=kvs)] = dk
        self_acc[pl.ds(tok * kvs + kv, tok, stride=kvs)] = dv

    self_out[...] = self_acc[...].astype(BF16)

    for kv in range(kvs):
        dq_own(kv).wait()

        def end_dq(i, c, kv=kv):
            dq_copy(kv, i).wait_send()
            dq_arrival(kv, i).wait_recv()
            return c

        lax.fori_loop(1, nh, end_dq, 0)

        def end_rs(i, c, kv=kv):
            rs_copy(kv, i).wait_send()
            rs_copy(kv, i).wait_recv()
            cart_acc[kv] += land[kv, i - 1].astype(F32)
            return c

        lax.fori_loop(1, ndp, end_rs, 0)
        for kind in range(2):
            cart_out[pl.ds(kind * kvs + kv, share, stride=2 * kvs)] = cart_acc[kv, kind]


def on_device(ndp, nh, queries, out_grad, self_keys, self_values, cart_keys, cart_values, segment_ids):
    tok, heads, dim = queries.shape
    kvs = self_keys.shape[1]
    cart = cart_keys.shape[0]
    keys = cart + tok
    width = heads // kvs
    share = cart // ndp
    piece = tok // nh
    step = 256
    vmem = pl.BlockSpec(memory_space=pltpu.VMEM)
    dma = pltpu.SemaphoreType.DMA
    query_grads, cart_part, self_part = pl.pallas_call(
        functools.partial(kernel, ndp, nh, kvs),
        out_shape=(
            jax.ShapeDtypeStruct((piece, nh * heads * dim), BF16),
            jax.ShapeDtypeStruct((share * 2 * kvs, dim), F32),
            jax.ShapeDtypeStruct((2 * tok * kvs, dim), BF16),
        ),
        in_specs=[vmem] * 7,
        out_specs=(pl.BlockSpec(memory_space=pl.ANY), vmem, vmem),
        scratch_shapes=[
            pltpu.VMEM((tok * width // step, tok, step), F32),
            pltpu.VMEM((kvs, keys, dim), BF16),
            pltpu.VMEM((kvs, keys, dim), BF16),
            pltpu.VMEM((cart * kvs, dim), F32),
            pltpu.VMEM((keys, step), F32),
            pltpu.VMEM((keys, step), F32),
            pltpu.VMEM((8, step), F32),
            pltpu.VMEM((step, dim), F32),
            pltpu.VMEM((keys, step), F32),
            pltpu.VMEM((keys, step), F32),
            pltpu.VMEM((8, step), F32),
            pltpu.VMEM((step, dim), F32),
            pltpu.VMEM((keys, width * tok), BF16),
            pltpu.VMEM((keys, width * tok), BF16),
            pltpu.VMEM((tok, heads * dim), BF16),
            pltpu.VMEM((kvs, ndp - 1, 2, share, dim), BF16),
            pltpu.VMEM((kvs, ndp - 1, 2, share, dim), BF16),
            pltpu.VMEM((kvs, 2, share, dim), F32),
            pltpu.VMEM((2 * tok * kvs, dim), F32),
            dma((kvs, nh - 1)),
            dma((kvs, nh - 1)),
            dma((kvs,)),
            dma((kvs, ndp - 1)),
            dma((kvs, ndp - 1)),
        ],
        compiler_params=pltpu.CompilerParams(
            collective_id=0, has_side_effects=True, vmem_limit_bytes=60 << 20
        ),
        name="attention_backward",
    )(
        segment_ids, queries, out_grad,
        cart_keys.reshape(cart * kvs, dim), cart_values.reshape(cart * kvs, dim),
        self_keys.reshape(tok * kvs, dim), self_values.reshape(tok * kvs, dim),
    )
    cart_grads = cart_part.reshape(share, 2, kvs, dim)
    self_grads = self_part.reshape(2, tok, kvs, dim)
    return cart_grads, self_grads, query_grads


def solution(mesh):
    in_specs = (
        P(("groups", "dp"), "heads", None),
        P(("groups", "dp"), "heads", None),
        P(("groups", "dp"), "heads", None),
        P(("groups", "dp"), "heads", None),
        P("groups", "heads", None),
        P("groups", "heads", None),
        P(("groups", "dp"), None),
    )
    out_specs = (
        P(("groups", "dp"), None, "heads", None),
        P(None, ("groups", "dp"), "heads", None),
        P(("groups", "dp", "heads"), None),
    )
    body = functools.partial(on_device, mesh.shape["dp"], mesh.shape["heads"])
    return jax.shard_map(body, mesh=mesh, in_specs=in_specs, out_specs=out_specs, check_vma=False)
```

time: 65.7 us -> 50.7 us (0.77)
  local copies, waits for them, and re-layouts: 12.6 us -> 4.91 us
  Pallas kernels: 51 us -> 45 us
  other arithmetic: 1.16 us -> 0 us
    pallas_call x1, Pallas kernels: 51 us -> 45 us  [on_device(): pl.pallas_call(functools.partial(kernel, ndp, nh, kvs), out_shape=(jax.Sh...]
    unnamed x15 -> x5, local copies, waits for them, and re-layouts: 9.16 us -> 4.91 us
    transpose x1 -> x0, local copies, waits for them, and re-layouts: 1.94 us -> none  [on_device(): g = out_grad.transpose(1, 0, 2)]
    reshape x1 -> x0, local copies, waits for them, and re-layouts: 1.48 us -> none  [on_device(): segment_ids.reshape(tok, 1)]
    transpose x1 -> x0, other arithmetic: 1.16 us -> none  [on_device(): k = jnp.concatenate([cart_keys, self_keys], axis=0).transpose(1, 0, 2)]
where the time goes in v1:
time: 50.7 us; the launch traced here: 50.6 us
  Pallas kernels  45 us (89%)
  local copies, waits for them, and re-layouts  4.91 us (10%)
  between operations  0.65 us (1%)
    pallas_call x1, Pallas kernels, on_device(): pl.pallas_call(functools.partial(kernel, ndp, nh, kvs), out_shape=(jax.Sh...  45 us
    unnamed x5, local copies, waits for them, and re-layouts  4.91 us

profile of v1, /device:TPU:0, one launch (start us, length us, event | category | flops | bytes accessed | tf_op | source)
XLA Modules:
  0.0 50.6 jit_solution(12550868308602284041)
XLA Ops:
  0.6 45.0 %attention_backward.1 = (bf16[64,8192]{1,0:T(8,128)(2,1)}, f32[1024,128]{1,0:T(8,128)}, bf16[1024,128]{1,0:T(8,128)(2,1)}) custom-call(s32[1,256]{1,0:T(1,128)} %seg_ref.1, bf16[256,16,128]{2,1,0:T(8,128)(2,1)} %q_ref.1, bf16[256,16,128]{2,1,0:T(8,128)(2,1)} %g_ref.1, bf16[2048,128]{1,0:T(8,128)(2,1)} %bitcast.6, bf16[2048,128]{1,0:T(8,128)(2,1)} %bitcast.7, ...), custom_call_target="tpu_custom_call" | custom-call | tf_op jit(solution)/shard_map/attention_backward/pallas_call | solution.py:250
  45.6 0.0 copy-start
  45.6 2.1 %copy.13 = f32[256,2,2,128]{3,2,1,0:T(2,128)} copy(f32[256,2,2,128]{3,2,1,0:T(2,128)} %bitcast.8) | data formatting | bytes 1048576
  47.7 1.8 %copy.14 = bf16[2,256,2,128]{3,2,1,0:T(2,128)(2,1)} copy(bf16[2,256,2,128]{3,2,1,0:T(2,128)(2,1)} %bitcast.9) | data formatting | bytes 524288
  49.6 0.0 copy-done
  49.6 1.0 %copy.15 = bf16[64,8192]{1,0:T(8,128)(2,1)} copy(bf16[64,8192]{1,0:T(8,128)(2,1)S(1)} %copy-done) | data formatting | bytes 2097152
Async XLA Ops:
  45.6 3.9 %copy-start = (bf16[64,8192]{1,0:T(8,128)(2,1)S(1)}, bf16[64,8192]{1,0:T(8,128)(2,1)}, u32[]{:S(2)}) copy-start(bf16[64,8192]{1,0:T(8,128)(2,1)} %get-tuple-element.14) | copy-start | bytes 3145732

commit v2 on v1

--- a/solution.py
+++ b/solution.py
@@ -11,6 +11,8 @@
 F32 = jnp.float32
 BF16 = jnp.bfloat16
 MASKED = -1e30
+CHUNK = 256
+FINE = 64
 MESH = pl.DeviceIdType.MESH
 
 
@@ -39,7 +41,8 @@
     step = s_a.shape[1]
     span = step // width
     blocks = tok // span
-    chunk = 128
+    chunk = CHUNK
+    fine = FINE
     scale = dim ** -0.5
     expo = scale * math.log2(math.e)
     my_dp = lax.axis_index("dp")
@@ -89,44 +92,61 @@
         heads_at = pl.ds(pl.multiple_of(kv * width, width), width)
         return ref[pl.ds(b * span, span), heads_at, :].reshape(step, dim)
 
+    def score_chunk(kv, b, lo, qb, gb, s_x, d_x, peak):
+        s = nt(k_scr[kv, lo : lo + chunk], qb)
+        if lo >= cart:
+            s = s + bias[b, lo - cart : lo - cart + chunk]
+        s_x[lo : lo + chunk] = s
+        top = jnp.max(s.reshape(chunk // 8, 8, step), axis=0)
+        d_x[lo : lo + chunk] = nt(v_scr[kv, lo : lo + chunk], gb)
+        return top if peak is None else jnp.maximum(peak, top)
+
+    def settle(peak, m_x):
+        m_x[...] = jnp.broadcast_to(jnp.max(peak, axis=0, keepdims=True), (8, step))
+
     def score(kv, b, s_x, d_x, m_x):
         qb = rows_of(q_ref, kv, b)
         gb = rows_of(g_ref, kv, b)
         peak = None
         for lo in range(0, keys, chunk):
-            s = nt(k_scr[kv, lo : lo + chunk], qb)
-            if lo >= cart:
-                s = s + bias[b, lo - cart : lo - cart + chunk]
-            s_x[lo : lo + chunk] = s
-            top = jnp.max(s.reshape(chunk // 8, 8, step), axis=0)
-            peak = top if peak is None else jnp.maximum(peak, top)
-            d_x[lo : lo + chunk] = nt(v_scr[kv, lo : lo + chunk], gb)
-        m_x[...] = jnp.broadcast_to(jnp.max(peak, axis=0, keepdims=True), (8, step))
-
-    def backward(kv, b, s_x, d_x, m_x, w_x):
+            peak = score_chunk(kv, b, lo, qb, gb, s_x, d_x, peak)
+        settle(peak, m_x)
+
+    def score_and_backward(kv_s, b_s, s_y, d_y, m_y, kv, b, s_x, d_x, m_x, w_x):
+        qb = rows_of(q_ref, kv_s, b_s)
+        gb = rows_of(g_ref, kv_s, b_s)
+        peak_y = None
         peak = m_x[:1]
         total = jnp.zeros((8, step), F32)
         mixed = jnp.zeros((8, step), F32)
         for lo in range(0, keys, chunk):
-            e = jnp.exp2((s_x[lo : lo + chunk] - peak) * expo)
-            s_x[lo : lo + chunk] = e
-            total = total + jnp.sum(e.reshape(chunk // 8, 8, step), axis=0)
-            ed = e * d_x[lo : lo + chunk]
-            mixed = mixed + jnp.sum(ed.reshape(chunk // 8, 8, step), axis=0)
+            peak_y = score_chunk(kv_s, b_s, lo, qb, gb, s_y, d_y, peak_y)
+            for at in range(lo, lo + chunk, fine):
+                e = jnp.exp2((s_x[at : at + fine] - peak) * expo)
+                s_x[at : at + fine] = e
+                total = total + jnp.sum(e.reshape(fine // 8, 8, step), axis=0)
+                ed = e * d_x[at : at + fine]
+                mixed = mixed + jnp.sum(ed.reshape(fine // 8, 8, step), axis=0)
+        settle(peak_y, m_y)
         inverse = 1.0 / jnp.sum(total, axis=0, keepdims=True)
         center = jnp.sum(mixed, axis=0, keepdims=True) * inverse
-        at = pl.ds(pl.multiple_of(b * step, step), step)
-        for lo in range(0, keys, chunk):
-            p = s_x[lo : lo + chunk] * inverse
-            p_scr[lo : lo + chunk, at] = p.astype(BF16)
-            ds_scr[lo : lo + chunk, at] = (p * (d_x[lo : lo + chunk] - center)).astype(BF16)
-        w_x[...] = tn(ds_scr[:, at], k_scr[kv]) * scale
+        here = pl.ds(pl.multiple_of(b * step, step), step)
+        dq = None
+        for lo in range(0, keys, 256):
+            for at in range(lo, lo + 256, fine):
+                p = s_x[at : at + fine] * inverse
+                p_scr[at : at + fine, here] = p.astype(BF16)
+                ds_scr[at : at + fine, here] = (p * (d_x[at : at + fine] - center)).astype(BF16)
+            part = tn(ds_scr[lo : lo + 256, here], k_scr[kv, lo : lo + 256])
+            dq = part if dq is None else dq + part
+        w_x[...] = dq * scale
         rows = pl.ds(pl.multiple_of(b * span, span), span)
         for hh in range(width):
             out = w_x[pl.ds(hh, span, stride=width)].astype(BF16)
             dq_buf[rows, kv * cols + hh * dim : kv * cols + (hh + 1) * dim] = out
 
     cols = width * dim
+    done = 2 * span // piece
 
     def dq_copy(kv, i):
         to = lax.rem(my_h + i, nh)
@@ -172,22 +192,29 @@
 
     for kv in range(kvs):
         def two_blocks(i, c, kv=kv):
-            score(kv, 2 * i + 1, s_b, d_b, m_b)
-            backward(kv, 2 * i, s_a, d_a, m_a, w_a)
+            score_and_backward(
+                kv, 2 * i + 1, s_b, d_b, m_b,
+                kv, 2 * i, s_a, d_a, m_a, w_a,
+            )
             after = kv * blocks + 2 * i + 2
-            score(jnp.minimum(after // blocks, kvs - 1), lax.rem(after, blocks), s_a, d_a, m_a)
-            backward(kv, 2 * i + 1, s_b, d_b, m_b, w_b)
+            score_and_backward(
+                jnp.minimum(after // blocks, kvs - 1), lax.rem(after, blocks), s_a, d_a, m_a,
+                kv, 2 * i + 1, s_b, d_b, m_b, w_b,
+            )
+            for t in range(done):
+                away = lax.rem(i * done + t - my_h + nh, nh)
+
+                @pl.when(away == 0)
+                def _():
+                    dq_own(kv).start()
+
+                @pl.when(away != 0)
+                def _():
+                    dq_copy(kv, away).start()
+
             return c
 
         lax.fori_loop(0, blocks // 2, two_blocks, 0)
-
-        dq_own(kv).start()
-
-        def send_dq(i, c, kv=kv):
-            dq_copy(kv, i).start()
-            return c
-
-        lax.fori_loop(1, nh, send_dq, 0)
 
         q_rows = q_ref[:, kv * width : (kv + 1) * width, :].reshape(width * tok, dim)
         g_rows = g_ref[:, kv * width : (kv + 1) * width, :].reshape(width * tok, dim)
@@ -234,6 +261,17 @@
         lax.fori_loop(1, ndp, end_rs, 0)
         for kind in range(2):
             cart_out[pl.ds(kind * kvs + kv, share, stride=2 * kvs)] = cart_acc[kv, kind]
+
+
+def finish(dq_in, cart_in, self_in, dq_out, cart_out, self_out, dq_buf, cart_buf, self_buf, sems):
+    trio = ((dq_in, dq_buf, dq_out), (cart_in, cart_buf, cart_out), (self_in, self_buf, self_out))
+    for n, (src, buf, _) in enumerate(trio):
+        pltpu.make_async_copy(src, buf, sems.at[0, n]).start()
+    for n, (src, buf, dst) in enumerate(trio):
+        pltpu.make_async_copy(src, buf, sems.at[0, n]).wait()
+        pltpu.make_async_copy(buf, dst, sems.at[1, n]).start()
+    for n, (_, buf, dst) in enumerate(trio):
+        pltpu.make_async_copy(buf, dst, sems.at[1, n]).wait()
 
 
 def on_device(ndp, nh, queries, out_grad, self_keys, self_values, cart_keys, cart_values, segment_ids):
@@ -291,6 +329,16 @@
         cart_keys.reshape(cart * kvs, dim), cart_values.reshape(cart * kvs, dim),
         self_keys.reshape(tok * kvs, dim), self_values.reshape(tok * kvs, dim),
     )
+    parts = (query_grads, cart_part, self_part)
+    anywhere = pl.BlockSpec(memory_space=pl.ANY)
+    query_grads, cart_part, self_part = pl.pallas_call(
+        finish,
+        out_shape=tuple(jax.ShapeDtypeStruct(x.shape, x.dtype) for x in parts),
+        in_specs=[anywhere] * 3,
+        out_specs=(anywhere,) * 3,
+        scratch_shapes=[pltpu.VMEM(x.shape, x.dtype) for x in parts] + [dma((2, 3))],
+        name="finish",
+    )(*parts)
     cart_grads = cart_part.reshape(share, 2, kvs, dim)
     self_grads = self_part.reshape(2, tok, kvs, dim)
     return cart_grads, self_grads, query_grads

time: 50.7 us -> 47.4 us (0.935)
  local copies, waits for them, and re-layouts: 4.91 us -> 0 us
  Pallas kernels: 45 us -> 46.6 us
    unnamed x5 -> x0, local copies, waits for them, and re-layouts: 4.91 us -> none
    pallas_call x0 -> x1, Pallas kernels: none -> 2.5 us  [on_device(): pl.pallas_call(finish, out_shape=tuple((jax.ShapeDtypeStruct(x.shape, x.d...]
    pallas_call x1, Pallas kernels: 45 us -> 44.2 us  [on_device(): pl.pallas_call(functools.partial(kernel, ndp, nh, kvs), out_shape=(jax.Sh...]
where the time goes in v2:
time: 47.4 us; the launch traced here: 47.3 us
  Pallas kernels  46.6 us (98%)
  between operations  0.64 us (1%)
    pallas_call x1, Pallas kernels, on_device(): pl.pallas_call(functools.partial(kernel, ndp, nh, kvs), out_shape=(jax.Sh...  44.2 us
    pallas_call x1, Pallas kernels, on_device(): pl.pallas_call(finish, out_shape=tuple((jax.ShapeDtypeStruct(x.shape, x.d...  2.5 us

profile of v2, /device:TPU:0, one launch (start us, length us, event | category | flops | bytes accessed | tf_op | source)
XLA Modules:
  0.0 47.3 jit_solution(10088676704119553102)
XLA Ops:
  0.6 44.2 %attention_backward.1 = (bf16[64,8192]{1,0:T(8,128)(2,1)}, f32[1024,128]{1,0:T(8,128)}, bf16[1024,128]{1,0:T(8,128)(2,1)}) custom-call(s32[1,256]{1,0:T(1,128)} %seg_ref.1, bf16[256,16,128]{2,1,0:T(8,128)(2,1)} %q_ref.1, bf16[256,16,128]{2,1,0:T(8,128)(2,1)} %g_ref.1, bf16[2048,128]{1,0:T(8,128)(2,1)} %bitcast.6, bf16[2048,128]{1,0:T(8,128)(2,1)} %bitcast.7, ...), custom_call_target="tpu_custom_call" | custom-call | tf_op jit(solution)/shard_map/attention_backward/pallas_call | solution.py:288
  44.8 2.5 %finish.1 = (bf16[64,8192]{1,0:T(8,128)(2,1)}, f32[1024,128]{1,0:T(8,128)}, bf16[1024,128]{1,0:T(8,128)(2,1)}) custom-call(bf16[64,8192]{1,0:T(8,128)(2,1)} %get-tuple-element.9.dq_in, f32[1024,128]{1,0:T(8,128)} %get-tuple-element.10.cart_in, bf16[1024,128]{1,0:T(8,128)(2,1)} %get-tuple-element.11.self_in), custom_call_target="tpu_custom_call" | custom-call | tf_op jit(solution)/shard_map/finish/pallas_call | solution.py:334

commit v3 on v2

--- a/solution.py
+++ b/solution.py
@@ -11,8 +11,8 @@
 F32 = jnp.float32
 BF16 = jnp.bfloat16
 MASKED = -1e30
-CHUNK = 256
-FINE = 64
+CHUNK = 128
+FINE = 32
 MESH = pl.DeviceIdType.MESH
 
 
@@ -192,15 +192,21 @@
 
     for kv in range(kvs):
         def two_blocks(i, c, kv=kv):
-            score_and_backward(
-                kv, 2 * i + 1, s_b, d_b, m_b,
-                kv, 2 * i, s_a, d_a, m_a, w_a,
-            )
-            after = kv * blocks + 2 * i + 2
-            score_and_backward(
-                jnp.minimum(after // blocks, kvs - 1), lax.rem(after, blocks), s_a, d_a, m_a,
-                kv, 2 * i + 1, s_b, d_b, m_b, w_b,
-            )
+            @pl.when(i >= 0)
+            def _():
+                score_and_backward(
+                    kv, 2 * i + 1, s_b, d_b, m_b,
+                    kv, 2 * i, s_a, d_a, m_a, w_a,
+                )
+
+            @pl.when(i < blocks)
+            def _():
+                after = kv * blocks + 2 * i + 2
+                score_and_backward(
+                    jnp.minimum(after // blocks, kvs - 1), lax.rem(after, blocks), s_a, d_a, m_a,
+                    kv, 2 * i + 1, s_b, d_b, m_b, w_b,
+                )
+
             for t in range(done):
                 away = lax.rem(i * done + t - my_h + nh, nh)
 

time: 47.4 us -> 44.1 us (0.930)
  Pallas kernels: 46.6 us -> 43.3 us
    pallas_call x1, Pallas kernels: 44.2 us -> 40.8 us  [on_device(): pl.pallas_call(functools.partial(kernel, ndp, nh, kvs), out_shape=(jax.Sh...]
where the time goes in v3:
time: 44.1 us; the launch traced here: 43.9 us
  Pallas kernels  43.3 us (98%)
  between operations  0.64 us (1%)
    pallas_call x1, Pallas kernels, on_device(): pl.pallas_call(functools.partial(kernel, ndp, nh, kvs), out_shape=(jax.Sh...  40.8 us
    pallas_call x1, Pallas kernels, on_device(): pl.pallas_call(finish, out_shape=tuple((jax.ShapeDtypeStruct(x.shape, x.d...  2.5 us

profile of v3, /device:TPU:0, one launch (start us, length us, event | category | flops | bytes accessed | tf_op | source)
XLA Modules:
  0.0 43.9 jit_solution(2139250174703742427)
XLA Ops:
  0.6 40.8 %attention_backward.1 = (bf16[64,8192]{1,0:T(8,128)(2,1)}, f32[1024,128]{1,0:T(8,128)}, bf16[1024,128]{1,0:T(8,128)(2,1)}) custom-call(s32[1,256]{1,0:T(1,128)} %seg_ref.1, bf16[256,16,128]{2,1,0:T(8,128)(2,1)} %q_ref.1, bf16[256,16,128]{2,1,0:T(8,128)(2,1)} %g_ref.1, bf16[2048,128]{1,0:T(8,128)(2,1)} %bitcast.6, bf16[2048,128]{1,0:T(8,128)(2,1)} %bitcast.7, ...), custom_call_target="tpu_custom_call" | custom-call | tf_op jit(solution)/shard_map/attention_backward/pallas_call | solution.py:294
  41.4 2.5 %finish.1 = (bf16[64,8192]{1,0:T(8,128)(2,1)}, f32[1024,128]{1,0:T(8,128)}, bf16[1024,128]{1,0:T(8,128)(2,1)}) custom-call(bf16[64,8192]{1,0:T(8,128)(2,1)} %get-tuple-element.9.dq_in, f32[1024,128]{1,0:T(8,128)} %get-tuple-element.10.cart_in, bf16[1024,128]{1,0:T(8,128)(2,1)} %get-tuple-element.11.self_in), custom_call_target="tpu_custom_call" | custom-call | tf_op jit(solution)/shard_map/finish/pallas_call | solution.py:340
